TPU v7x, 512 devices: a whole 4x4x16 slice. The times are simulated.
512 devices in a mesh: dp: 8 (over y, core), expert: 64 (over x, z).
Axes of the slice: x: 4, y: 4, z: 16, core: 2. Of those that a mesh axis runs over, the one named last changes fastest.
Arguments:
- layer_in: bfloat16 [2048, 4096], P('expert', 'dp'), may hold values from -6 to 6
- grad_out: bfloat16 [2048, 4096], P('expert', 'dp'), may hold values from -6 to 6
- gate_prob: float32 [2048, 8], P('expert'), may hold values from 0.05 to 0.6
- expert_ids: int32 [2048, 8], P('expert'), may hold values from 0 to 31, as said below
- replica_index: int32 [2048, 8], P('expert'), may hold values from 0 to 3, as said below
- slot_expert: int32 [64], replicated, may hold values from 0 to 31, as said below
- w_gate: bfloat16 [64, 4096, 1024], P('expert', None, 'dp')
- w_up: bfloat16 [64, 4096, 1024], P('expert', None, 'dp')
- w_down: bfloat16 [64, 1024, 4096], P('expert', 'dp')
Outputs:
- grad_in: bfloat16 [2048, 4096], P('expert', 'dp')
- grad_w_down: bfloat16 [64, 1024, 4096], P('expert', 'dp')
Inputs may be any that keep to these rules, and one draw needn't show every extreme that they name: `slot_expert`: every expert owns one run of consecutive slots, counted cyclically (slot 63 is followed by slot 0), of 1 to 4 slots; the runs cover all 64 slots. `expert_ids`: the 8 experts of one token are different. `replica_index`: each entry is below the number of slots of the expert of the same choice. Of the 32 tokens of one index of expert, at most 8 choices go to any one slot, and in every draw some slot receives exactly 8 from the tokens of every index of expert.
All inputs are finite; a program needn't handle non-finite values.
Results may differ from a plain program's by a relative error of at most 0.014.
Values may be sent and summed in bfloat16 or wider, within the bound.
No kernel may reach another device: no remote copies, remote signals or barrier semaphores. Data moves between devices by JAX's collectives and lax.ppermute only.
A program may use at most 64 MiB of HBM per device.

v0:
```python
import jax
import jax.numpy as jnp
from jax import lax
from jax.sharding import PartitionSpec as P

TOP = 8


def passed_along(value, axis, steps):
    count = lax.axis_size(axis)
    pairs = [(source, (source + steps) % count) for source in range(count)]
    return lax.ppermute(value, axis, pairs)


def body(
    layer_in, grad_out, gate_prob, expert_ids, replica_index, slot_expert, w_gate, w_up, w_down
):
    slots = lax.axis_size("expert")
    maxrep = min(4, slots // 8)
    tok_count = layer_in.shape[0]
    capacity = tok_count // maxrep
    recv_rows = slots * capacity
    expert_count = (8 - maxrep) * slots // 8
    slot_index = jnp.arange(slots, dtype=jnp.int32)
    expert_index = jnp.arange(expert_count, dtype=jnp.int32)
    is_start = slot_expert != jnp.roll(slot_expert, 1)
    first_slot = jnp.sum(
        jnp.where(
            (slot_expert[None, :] == expert_index[:, None]) & is_start[None, :],
            slot_index[None, :],
            0,
        ),
        axis=1,
    )
    own_index = lax.axis_index("expert")

    def route(ids, replicas):
        first = jnp.sum(jnp.where(ids[..., None] == expert_index, first_slot, 0), axis=-1)
        return (first + replicas) % slots

    codes = (expert_ids * 8 + replica_index).astype(jnp.float32)
    words = jnp.concatenate([codes, gate_prob], axis=1)
    all_words = lax.all_gather(words, "expert", axis=0, tiled=True)
    all_codes = all_words[:, :TOP].astype(jnp.int32)
    all_prob = all_words[:, TOP:]
    all_inputs = lax.all_gather(layer_in, "expert", axis=0, tiled=True)
    all_grads = lax.all_gather(grad_out, "expert", axis=0, tiled=True)
    here = route(all_codes // 8, all_codes % 8) == own_index
    prob_here = jnp.sum(jnp.where(here, all_prob, 0.0), axis=1)
    chosen = jnp.any(here, axis=1).astype(jnp.int32).reshape(slots, tok_count)
    rank = jnp.cumsum(chosen, axis=1) - chosen
    row = jnp.where(chosen > 0, slot_index[:, None] * capacity + rank, -1).reshape(-1)
    pick = (jnp.arange(recv_rows, dtype=jnp.int32)[:, None] == row[None, :]).astype(jnp.bfloat16)

    def picked(values):
        rows = jnp.dot(pick, values, preferred_element_type=jnp.float32).astype(jnp.bfloat16)
        return lax.all_gather(rows, "dp", axis=1, tiled=True)

    inputs = picked(all_inputs)
    scaled = picked((prob_here[:, None] * all_grads.astype(jnp.float32)).astype(jnp.bfloat16))
    width = inputs.shape[1]
    gate_matrix = w_gate[0]
    up_matrix = w_up[0]
    down_matrix = w_down[0]
    gate_pre = jnp.dot(inputs, gate_matrix, preferred_element_type=jnp.float32)
    up_pre = jnp.dot(inputs, up_matrix, preferred_element_type=jnp.float32)
    hidden = (jax.nn.silu(gate_pre) * up_pre).astype(jnp.bfloat16)
    contract_last = (((1,), (1,)), ((), ()))
    hidden_grad = lax.dot_general(
        scaled, down_matrix, contract_last, preferred_element_type=jnp.float32
    )
    sigma = jax.nn.sigmoid(gate_pre)
    gate_grad = (hidden_grad * up_pre * sigma * (1.0 + gate_pre * (1.0 - sigma))).astype(
        jnp.bfloat16
    )
    up_grad = (hidden_grad * gate_pre * sigma).astype(jnp.bfloat16)
    partial_value = lax.dot_general(
        gate_grad, gate_matrix, contract_last, preferred_element_type=jnp.float32
    )
    partial_value = partial_value + lax.dot_general(
        up_grad, up_matrix, contract_last, preferred_element_type=jnp.float32
    )
    partial_value = partial_value.reshape(slots, capacity, width)
    summed = lax.psum_scatter(
        partial_value.astype(jnp.bfloat16), "dp", scatter_dimension=2, tiled=True
    )
    returned = lax.all_to_all(summed, "expert", split_axis=0, concat_axis=0, tiled=True)
    flat_back = returned.reshape(recv_rows, -1)
    route_slot = route(expert_ids, replica_index)
    onehot = jnp.any(route_slot[:, :, None] == slot_index, axis=1).astype(jnp.int32)
    rank_back = jnp.cumsum(onehot, axis=0) - onehot
    place = jnp.arange(capacity, dtype=jnp.int32)
    unpick = ((onehot[:, :, None] > 0) & (rank_back[:, :, None] == place)).astype(jnp.bfloat16)
    grad_in = jnp.dot(
        unpick.reshape(tok_count, recv_rows), flat_back, preferred_element_type=jnp.float32
    ).astype(jnp.bfloat16)
    slot_partial = lax.dot_general(
        hidden, scaled, (((0,), (0,)), ((), ())), preferred_element_type=jnp.float32
    ).astype(jnp.bfloat16)
    expert_here = jnp.sum(jnp.where(slot_index == own_index, slot_expert, 0))

    def same_at(offset):
        neighbour = (own_index - offset) % slots
        match = jnp.any((slot_index == neighbour) & (slot_expert == expert_here))
        return match.astype(jnp.float32)

    own = slot_partial.astype(jnp.float32)
    left = own + same_at(1) * passed_along(slot_partial, "expert", 1).astype(jnp.float32)
    right = own + same_at(-1) * passed_along(slot_partial, "expert", -1).astype(jnp.float32)
    far_left = passed_along(left.astype(jnp.bfloat16), "expert", 2).astype(jnp.float32)
    far_right = passed_along(right.astype(jnp.bfloat16), "expert", -2).astype(jnp.float32)
    total = left + same_at(2) * far_left + (right - own) + same_at(-2) * far_right
    grad_w_down = total.astype(jnp.bfloat16)[None]
    return (grad_in, grad_w_down)


def solution(mesh):
    placed = (
        P("expert", "dp"),
        P("expert", "dp"),
        P("expert", None),
        P("expert", None),
        P("expert", None),
        P(),
        P("expert", None, "dp"),
        P("expert", None, "dp"),
        P("expert", "dp", None),
    )
    return jax.shard_map(
        body,
        mesh=mesh,
        in_specs=placed,
        out_specs=(P("expert", "dp"), P("expert", "dp", None)),
        check_vma=False,
    )
```

profile of v0, /device:TPU:6, one launch (start us, length us, event | category | flops | bytes accessed | tf_op | source)
XLA Modules:
  0.0 514.9 jit_solution(13106250262551552550)
XLA Ops:
  11.4 106.0 %all-gather = f32[64,32,16]{1,2,0:T(8,128)S(1)} all-gather(f32[1,32,16]{1,2,0:T(8,128)S(1)} %maximum_bitcast_fusion), channel_id=1, replica_groups=mesh['dp'=8,'expert'=64] {'expert'}, dimensions={0}, use_global_device_ids=true | all-gather | bytes 133120 | tf_op jit(solution)/shard_map/all_gather | solution.py:43
  118.4 1.4 broadcast_compare_fusion
  121.0 34.1 %all-gather.10.cloned.1.call-done = bf16[2048,512]{1,0:T(8,128)(2,1)} async-done(((bf16[32,512]{1,0:T(8,128)(2,1)}), bf16[2048,512]{1,0:T(8,128)(2,1)}) %all-gather.10.cloned.1.call-update) | async-done | bytes 2097168 | tf_op jit(solution)/shard_map/all_gather | solution.py:46
  155.1 3.6 fusion.12
  158.8 136.2 %all-gather.6.cloned.1.call-done = bf16[2048,512]{1,0:T(8,128)(2,1)} async-done(((bf16[32,512]{1,0:T(8,128)(2,1)}), bf16[2048,512]{1,0:T(8,128)(2,1)}) %all-gather.6.cloned.1.call-update) | async-done | bytes 2097168 | tf_op jit(solution)/shard_map/all_gather | solution.py:47
  295.1 3.8 fusion.11
  298.9 35.9 %all-gather.12.cloned.1.call-done = bf16[512,4096]{1,0:T(8,128)(2,1)} async-done(((bf16[512,512]{1,0:T(8,128)(2,1)}), bf16[512,4096]{1,0:T(8,128)(2,1)}) %all-gather.12.cloned.1.call-update) | async-done | bytes 4194320 | tf_op jit(solution)/shard_map/all_gather | solution.py:57
  334.9 3.6 fusion.16
  339.7 37.0 %all-gather.8.cloned.1.call-done = bf16[512,4096]{1,0:T(8,128)(2,1)} async-done(((bf16[512,512]{1,0:T(8,128)(2,1)}), bf16[512,4096]{1,0:T(8,128)(2,1)}) %all-gather.8.cloned.1.call-update) | async-done | bytes 4194320 | tf_op jit(solution)/shard_map/all_gather | solution.py:57
  376.7 3.7 fusion.21
  381.7 3.2 fusion
  384.9 3.0 convolution_convert_fusion
  387.9 3.5 collective-permute-start
  391.4 4.7 collective-permute-start.2
  398.2 19.6 %collective-permute-done = bf16[128,4096]{1,0:T(8,128)(2,1)S(1)} collective-permute-done((bf16[128,4096]{1,0:T(8,128)(2,1)S(1)}, bf16[128,4096]{1,0:T(8,128)(2,1)S(1)}, u32[]{:S(2)}, u32[]{:S(2)}) %collective-permute-start) | collective-permute-done | bytes 1048608 | tf_op jit(solution)/shard_map/ppermute | solution.py:12
  418.9 3.2 fusion.7
  422.1 5.2 %collective-permute-start.1 = (bf16[128,4096]{1,0:T(8,128)(2,1)}, bf16[128,4096]{1,0:T(8,128)(2,1)}, u32[]{:S(2)}, u32[]{:S(2)}) collective-permute-start(bf16[128,4096]{1,0:T(8,128)(2,1)} %get-tuple-element.10), channel_id=1, source_target_pairs={{0,2},{1,3},{2,4},{3,5},{4,6},{5,7},{6,8},{7,9},{8,10},{9,11},{10,... | collective-permute-start | bytes 3145736 | tf_op jit(solution)/shard_map/ppermute | solution.py:12
  427.3 3.7 collective-permute-start.3
  431.0 16.0 %all-to-all-start = ((bf16[64,8,512]{2,1,0:T(8,128)(2,1)}), bf16[64,8,512]{2,1,0:T(8,128)(2,1)}, u32[]{:S(2)}, u32[]{:S(2)}) async-start(bf16[64,8,512]{2,1,0:T(8,128)(2,1)} %reduce-scatter.2.cloned.1.call-done), calls=%async_computation.1 | async-start | bytes 1048576 | tf_op jit(solution)/shard_map/all_to_all | solution.py:87
  449.4 10.2 %collective-permute-done.1 = bf16[128,4096]{1,0:T(8,128)(2,1)} collective-permute-done((bf16[128,4096]{1,0:T(8,128)(2,1)}, bf16[128,4096]{1,0:T(8,128)(2,1)}, u32[]{:S(2)}, u32[]{:S(2)}) %collective-permute-start.1) | collective-permute-done | bytes 1048608 | tf_op jit(solution)/shard_map/ppermute | solution.py:12
  459.6 9.6 %collective-permute-done.3 = bf16[128,4096]{1,0:T(8,128)(2,1)} collective-permute-done((bf16[128,4096]{1,0:T(8,128)(2,1)}, bf16[128,4096]{1,0:T(8,128)(2,1)}, u32[]{:S(2)}, u32[]{:S(2)}) %collective-permute-start.3) | collective-permute-done | bytes 1048608 | tf_op jit(solution)/shard_map/ppermute | solution.py:12
  469.1 3.9 fusion.23
  473.0 33.4 %all-to-all-done = bf16[64,8,512]{2,1,0:T(8,128)(2,1)} async-done(((bf16[64,8,512]{2,1,0:T(8,128)(2,1)}), bf16[64,8,512]{2,1,0:T(8,128)(2,1)}, u32[]{:S(2)}, u32[]{:S(2)}) %all-to-all-start) | async-done | bytes 524320 | tf_op jit(solution)/shard_map/all_to_all | solution.py:87
  506.4 1.9 fusion.13
  (54 shorter events, 12.1 us)
Async XLA Ops:
  7.2 327.7 %copy-start = (bf16[1,4096,128]{2,1,0:T(8,128)(2,1)S(1)}, bf16[1,4096,128]{2,1,0:T(8,128)(2,1)}, u32[]{:S(2)}) copy-start(bf16[1,4096,128]{2,1,0:T(8,128)(2,1)} %param.15) | copy-start | bytes 3145732
  7.2 110.6 %copy-start.5 = (s32[64]{0:T(128)S(1)}, s32[64]{0:T(128)}, u32[]{:S(2)}) copy-start(s32[64]{0:T(128)} %param.14) | copy-start | bytes 772
  7.2 147.9 %all-gather.10.cloned.1.call-start = ((), (), s32[]{:S(2)}) async-start(), calls=%async_computation.4 | async-start | bytes 2129920 | tf_op jit(solution)/shard_map/all_gather | solution.py:46
  7.9 287.1 %all-gather.6.cloned.1.call-start = ((), (), s32[]{:S(2)}) async-start(), calls=%async_computation.2 | async-start | bytes 2129920 | tf_op jit(solution)/shard_map/all_gather | solution.py:47
  8.7 326.2 %all-gather.12.cloned.1.call-start = ((), (), s32[]{:S(2)}) async-start(), calls=%async_computation.5 | async-start | bytes 4718592 | tf_op jit(solution)/shard_map/all_gather | solution.py:57
  158.8 217.9 %all-gather.8.cloned.1.call-start = ((), (), s32[]{:S(2)}) async-start(), calls=%async_computation.3 | async-start | bytes 4718592 | tf_op jit(solution)/shard_map/all_gather | solution.py:57
  298.9 39.6 %copy-start.2 = (bf16[1,4096,128]{2,1,0:T(8,128)(2,1)S(1)}, bf16[1,4096,128]{2,1,0:T(8,128)(2,1)}, u32[]{:S(2)}) copy-start(bf16[1,4096,128]{2,1,0:T(8,128)(2,1)} %param.16) | copy-start | bytes 3145732
  298.9 132.1 %reduce-scatter.2.cloned.1.call-start = ((), (), s32[]{:S(2)}) async-start(), calls=%async_computation.6 | async-start | bytes 4718592 | tf_op jit(solution)/shard_map/reduce_scatter | solution.py:84
  334.9 3.6 copy-start.1
  387.9 29.8 %collective-permute-start = (bf16[128,4096]{1,0:T(8,128)(2,1)S(1)}, bf16[128,4096]{1,0:T(8,128)(2,1)S(1)}, u32[]{:S(2)}, u32[]{:S(2)}) collective-permute-start(bf16[128,4096]{1,0:T(8,128)(2,1)S(1)} %convolution_convert_fusion), channel_id=1, source_target_pairs={{0,1},{1,2},{2,3},{3,4},{4,5},{5,6},{6,7},{7,8},{8,9},{9,10},{10,1... | collective-permute-start | bytes 3145736 | tf_op jit(solution)/shard_map/ppermute | solution.py:12
  391.4 27.5 %collective-permute-start.2 = (bf16[128,4096]{1,0:T(8,128)(2,1)S(1)}, bf16[128,4096]{1,0:T(8,128)(2,1)}, u32[]{:S(2)}, u32[]{:S(2)}) collective-permute-start(bf16[128,4096]{1,0:T(8,128)(2,1)S(1)} %convolution_convert_fusion), channel_id=1, source_target_pairs={{0,63},{1,0},{2,1},{3,2},{4,3},{5,4},{6,5},{7,6},{8,7},{9,8},{10,9... | collective-permute-start | bytes 3145736 | tf_op jit(solution)/shard_map/ppermute | solution.py:12
  398.1 48.9 %copy-start.3 = (s32[32,8]{0,1:T(8,128)S(1)}, s32[32,8]{0,1:T(8,128)}, u32[]{:S(2)}) copy-start(s32[32,8]{0,1:T(8,128)} %param.12) | copy-start | bytes 3076
  398.2 48.9 %copy-start.4 = (s32[32,8]{0,1:T(8,128)S(1)}, s32[32,8]{0,1:T(8,128)}, u32[]{:S(2)}) copy-start(s32[32,8]{0,1:T(8,128)} %param.13) | copy-start | bytes 3076
  422.1 37.5 %collective-permute-start.1 = (bf16[128,4096]{1,0:T(8,128)(2,1)}, bf16[128,4096]{1,0:T(8,128)(2,1)}, u32[]{:S(2)}, u32[]{:S(2)}) collective-permute-start(bf16[128,4096]{1,0:T(8,128)(2,1)} %get-tuple-element.10), channel_id=1, source_target_pairs={{0,2},{1,3},{2,4},{3,5},{4,6},{5,7},{6,8},{7,9},{8,10},{9,11},{10,... | collective-permute-start | bytes 3145736 | tf_op jit(solution)/shard_map/ppermute | solution.py:12
  427.3 41.9 %collective-permute-start.3 = (bf16[128,4096]{1,0:T(8,128)(2,1)}, bf16[128,4096]{1,0:T(8,128)(2,1)}, u32[]{:S(2)}, u32[]{:S(2)}) collective-permute-start(bf16[128,4096]{1,0:T(8,128)(2,1)} %get-tuple-element.11), channel_id=1, source_target_pairs={{0,62},{1,63},{2,0},{3,1},{4,2},{5,3},{6,4},{7,5},{8,6},{9,7},{10,... | collective-permute-start | bytes 3145736 | tf_op jit(solution)/shard_map/ppermute | solution.py:12
  431.0 75.5 %all-to-all-start = ((bf16[64,8,512]{2,1,0:T(8,128)(2,1)}), bf16[64,8,512]{2,1,0:T(8,128)(2,1)}, u32[]{:S(2)}, u32[]{:S(2)}) async-start(bf16[64,8,512]{2,1,0:T(8,128)(2,1)} %reduce-scatter.2.cloned.1.call-done), calls=%async_computation.1 | async-start | bytes 1048576 | tf_op jit(solution)/shard_map/all_to_all | solution.py:87
Sparse Core Ops, SparseCore 0:
  11.0 144.1 all-gather.9
  158.1 136.9 all-gather.5
  297.8 37.0 all-gather.11
  336.8 39.8 all-gather.7
  385.1 45.8 reduce-scatter.1
where the time goes:
time: 516 us; the launch traced here: 515 us
  waiting for transfers between devices  319 us (62%)
  blocking collectives  106 us (21%)
  starting transfers between devices  33.2 us (6%)
  matrix products  25.4 us (5%)
  between operations  16.6 us (3%)
  other arithmetic  13 us (3%)
    all_gather x1, waiting for transfers between devices, body(): all_grads = lax.all_gather(grad_out, 'expert', axis=0, tiled=True)  136 us
    all_gather x1, blocking collectives, body(): all_words = lax.all_gather(words, 'expert', axis=0, tiled=True)  106 us
    all_gather x2, waiting for transfers between devices, picked(): return lax.all_gather(rows, 'dp', axis=1, tiled=True)  72.9 us
    ppermute x4, waiting for transfers between devices, passed_along(): return lax.ppermute(value, axis, pairs)  40.5 us
    all_gather x1, waiting for transfers between devices, body(): all_inputs = lax.all_gather(layer_in, 'expert', axis=0, tiled=True)  34.1 us
    all_to_all x1, waiting for transfers between devices, body(): lax.all_to_all(summed, 'expert', split_axis=0, concat_axis=0, tiled=True)  33.4 us
    ppermute x4, starting transfers between devices, passed_along(): return lax.ppermute(value, axis, pairs)  17 us
    all_to_all x1, starting transfers between devices, body(): lax.all_to_all(summed, 'expert', split_axis=0, concat_axis=0, tiled=True)  16 us
  transfers between devices with their start and end apart: 10, of which 9 were waited for; matrix products, arithmetic and copies ran while one was open for 6% of the time, Pallas kernels for 0%

commit v1 on v0

--- a/solution.py
+++ b/solution.py
@@ -43,8 +43,11 @@
     all_words = lax.all_gather(words, "expert", axis=0, tiled=True)
     all_codes = all_words[:, :TOP].astype(jnp.int32)
     all_prob = all_words[:, TOP:]
-    all_inputs = lax.all_gather(layer_in, "expert", axis=0, tiled=True)
-    all_grads = lax.all_gather(grad_out, "expert", axis=0, tiled=True)
+    all_inputs, all_grads = jnp.split(
+        lax.all_gather(jnp.concatenate([layer_in, grad_out], axis=1), "expert", axis=0, tiled=True),
+        [layer_in.shape[1]],
+        axis=1,
+    )
     here = route(all_codes // 8, all_codes % 8) == own_index
     prob_here = jnp.sum(jnp.where(here, all_prob, 0.0), axis=1)
     chosen = jnp.any(here, axis=1).astype(jnp.int32).reshape(slots, tok_count)

time: 516 us -> 382 us (0.74)
  waiting for transfers between devices: 319 us -> 183 us
    all_gather x2 -> x1, waiting for transfers between devices: 170 us -> 39.5 us  [body(): lax.all_gather(jnp.concatenate([layer_in, grad_out], axis=1), 'expert', a...]
    all_to_all x1, waiting for transfers between devices: 33.4 us -> 20.7 us  [body(): lax.all_to_all(summed, 'expert', split_axis=0, concat_axis=0, tiled=True)]
    ppermute x4, waiting for transfers between devices: 40.5 us -> 53.1 us  [passed_along(): return lax.ppermute(value, axis, pairs)]
  transfers between devices with their start and end apart: 10 -> 9, of which waited for: 9 -> 8; matrix products, arithmetic and copies ran while one was open for 6% -> 7% of each run, Pallas kernels for 0% -> 0%
where the time goes in v1:
time: 382 us; the launch traced here: 381 us
  waiting for transfers between devices  183 us (48%)
  blocking collectives  106 us (28%)
  starting transfers between devices  33.4 us (9%)
  matrix products  25.4 us (7%)
  between operations  16.6 us (4%)
  other arithmetic  14.5 us (4%)
    all_gather x1, blocking collectives, body(): all_words = lax.all_gather(words, 'expert', axis=0, tiled=True)  106 us
    all_gather x2, waiting for transfers between devices, picked(): return lax.all_gather(rows, 'dp', axis=1, tiled=True)  69.8 us
    ppermute x4, waiting for transfers between devices, passed_along(): return lax.ppermute(value, axis, pairs)  53.1 us
    all_gather x1, waiting for transfers between devices, body(): lax.all_gather(jnp.concatenate([layer_in, grad_out], axis=1), 'expert', a...  39.5 us
    all_to_all x1, waiting for transfers between devices, body(): lax.all_to_all(summed, 'expert', split_axis=0, concat_axis=0, tiled=True)  20.7 us
    ppermute x4, starting transfers between devices, passed_along(): return lax.ppermute(value, axis, pairs)  17.2 us
    all_to_all x1, starting transfers between devices, body(): lax.all_to_all(summed, 'expert', split_axis=0, concat_axis=0, tiled=True)  16 us
  transfers between devices with their start and end apart: 9, of which 8 were waited for; matrix products, arithmetic and copies ran while one was open for 7% of the time, Pallas kernels for 0%

profile of v1, /device:TPU:6, one launch (start us, length us, event | category | flops | bytes accessed | tf_op | source)
XLA Modules:
  0.0 381.0 jit_solution(16876403359934506211)
XLA Ops:
  7.2 1.5 pad_maximum_fusion
  11.4 105.9 %all-gather = f32[64,32,16]{1,2,0:T(8,128)S(1)} all-gather(f32[1,32,16]{1,2,0:T(8,128)S(1)} %maximum_bitcast_fusion), channel_id=1, replica_groups=mesh['dp'=8,'expert'=64] {'expert'}, dimensions={0}, use_global_device_ids=true | all-gather | bytes 133120 | tf_op jit(solution)/shard_map/all_gather | solution.py:43
  118.4 1.3 broadcast_compare_fusion
  121.0 39.5 %all-gather.5.cloned.1.call-done = bf16[2048,1024]{1,0:T(8,128)(2,1)} async-done(((bf16[32,1024]{1,0:T(8,128)(2,1)}), bf16[2048,1024]{1,0:T(8,128)(2,1)}) %all-gather.5.cloned.1.call-update) | async-done | bytes 4194320 | tf_op jit(solution)/shard_map/all_gather | solution.py:47
  160.6 3.6 fusion.14
  164.3 3.8 fusion.13
  168.1 32.7 %all-gather.9.cloned.1.call-done = bf16[512,4096]{1,0:T(8,128)(2,1)} async-done(((bf16[512,512]{1,0:T(8,128)(2,1)}), bf16[512,4096]{1,0:T(8,128)(2,1)}) %all-gather.9.cloned.1.call-update) | async-done | bytes 4194320 | tf_op jit(solution)/shard_map/all_gather | solution.py:60
  200.8 3.6 fusion.20
  205.7 37.1 %all-gather.7.cloned.1.call-done = bf16[512,4096]{1,0:T(8,128)(2,1)} async-done(((bf16[512,512]{1,0:T(8,128)(2,1)}), bf16[512,4096]{1,0:T(8,128)(2,1)}) %all-gather.7.cloned.1.call-update) | async-done | bytes 4194320 | tf_op jit(solution)/shard_map/all_gather | solution.py:60
  242.8 3.7 fusion.25
  247.8 3.2 fusion
  251.1 3.0 convolution_convert_fusion
  254.0 3.5 collective-permute-start
  257.5 4.9 %collective-permute-start.2 = (bf16[128,4096]{1,0:T(8,128)(2,1)S(1)}, bf16[128,4096]{1,0:T(8,128)(2,1)}, u32[]{:S(2)}, u32[]{:S(2)}) collective-permute-start(bf16[128,4096]{1,0:T(8,128)(2,1)S(1)} %convolution_convert_fusion), channel_id=1, source_target_pairs={{0,63},{1,0},{2,1},{3,2},{4,3},{5,4},{6,5},{7,6},{8,7},{9,8},{10,9... | collective-permute-start | bytes 3145736 | tf_op jit(solution)/shard_map/ppermute | solution.py:12
  264.5 19.4 %collective-permute-done = bf16[128,4096]{1,0:T(8,128)(2,1)S(1)} collective-permute-done((bf16[128,4096]{1,0:T(8,128)(2,1)S(1)}, bf16[128,4096]{1,0:T(8,128)(2,1)S(1)}, u32[]{:S(2)}, u32[]{:S(2)}) %collective-permute-start) | collective-permute-done | bytes 1048608 | tf_op jit(solution)/shard_map/ppermute | solution.py:12
  285.0 3.2 fusion.9
  288.2 5.0 %collective-permute-start.1 = (bf16[128,4096]{1,0:T(8,128)(2,1)}, bf16[128,4096]{1,0:T(8,128)(2,1)}, u32[]{:S(2)}, u32[]{:S(2)}) collective-permute-start(bf16[128,4096]{1,0:T(8,128)(2,1)} %get-tuple-element.10), channel_id=1, source_target_pairs={{0,2},{1,3},{2,4},{3,5},{4,6},{5,7},{6,8},{7,9},{8,10},{9,11},{10,... | collective-permute-start | bytes 3145736 | tf_op jit(solution)/shard_map/ppermute | solution.py:12
  293.2 3.9 %collective-permute-start.3 = (bf16[128,4096]{1,0:T(8,128)(2,1)}, bf16[128,4096]{1,0:T(8,128)(2,1)}, u32[]{:S(2)}, u32[]{:S(2)}) collective-permute-start(bf16[128,4096]{1,0:T(8,128)(2,1)} %get-tuple-element.11), channel_id=1, source_target_pairs={{0,62},{1,63},{2,0},{3,1},{4,2},{5,3},{6,4},{7,5},{8,6},{9,7},{10,... | collective-permute-start | bytes 3145736 | tf_op jit(solution)/shard_map/ppermute | solution.py:12
  297.1 16.0 %all-to-all-start = ((bf16[64,8,512]{2,1,0:T(8,128)(2,1)}), bf16[64,8,512]{2,1,0:T(8,128)(2,1)}, u32[]{:S(2)}, u32[]{:S(2)}) async-start(bf16[64,8,512]{2,1,0:T(8,128)(2,1)} %reduce-scatter.2.cloned.1.call-done), calls=%async_computation.1 | async-start | bytes 1048576 | tf_op jit(solution)/shard_map/all_to_all | solution.py:90
  315.5 9.9 %collective-permute-done.1 = bf16[128,4096]{1,0:T(8,128)(2,1)} collective-permute-done((bf16[128,4096]{1,0:T(8,128)(2,1)}, bf16[128,4096]{1,0:T(8,128)(2,1)}, u32[]{:S(2)}, u32[]{:S(2)}) %collective-permute-start.1) | collective-permute-done | bytes 1048608 | tf_op jit(solution)/shard_map/ppermute | solution.py:12
  325.4 22.6 %collective-permute-done.3 = bf16[128,4096]{1,0:T(8,128)(2,1)} collective-permute-done((bf16[128,4096]{1,0:T(8,128)(2,1)}, bf16[128,4096]{1,0:T(8,128)(2,1)}, u32[]{:S(2)}, u32[]{:S(2)}) %collective-permute-start.3) | collective-permute-done | bytes 1048608 | tf_op jit(solution)/shard_map/ppermute | solution.py:12
  348.0 3.9 %fusion.27 = bf16[1,128,4096]{2,1,0:T(8,128)(2,1)} fusion(bf16[128,4096]{1,0:T(8,128)(2,1)} %collective-permute-done.3, f32[]{:T(128)S(6)} %convert_element_type.129, bf16[128,4096]{1,0:T(8,128)(2,1)} %collective-permute-done.2, f32[]{:T(128)S(6)} %convert_element_type.127, bf16[128,4096]{1,0:T(8,128)(2,1)} %collective-permute-done.1, ...), kind=kLoop, calls=%fused_computation.35 | loop fusion | flops 8388608 | bytes 6291472 | tf_op jit(solution)/shard_map/broadcast_in_dim | solution.py:116
  351.9 20.7 %all-to-all-done = bf16[64,8,512]{2,1,0:T(8,128)(2,1)} async-done(((bf16[64,8,512]{2,1,0:T(8,128)(2,1)}), bf16[64,8,512]{2,1,0:T(8,128)(2,1)}, u32[]{:S(2)}, u32[]{:S(2)}) %all-to-all-start) | async-done | bytes 524320 | tf_op jit(solution)/shard_map/all_to_all | solution.py:90
  372.5 1.9 fusion.17
  (52 shorter events, 10.7 us)
Async XLA Ops:
  7.2 193.7 %copy-start = (bf16[1,4096,128]{2,1,0:T(8,128)(2,1)S(1)}, bf16[1,4096,128]{2,1,0:T(8,128)(2,1)}, u32[]{:S(2)}) copy-start(bf16[1,4096,128]{2,1,0:T(8,128)(2,1)} %param.15) | copy-start | bytes 3145732
  7.2 110.6 %copy-start.5 = (s32[64]{0:T(128)S(1)}, s32[64]{0:T(128)}, u32[]{:S(2)}) copy-start(s32[64]{0:T(128)} %param.14) | copy-start | bytes 772
  7.2 153.4 %all-gather.5.cloned.1.call-start = ((), (), s32[]{:S(2)}) async-start(), calls=%async_computation.2 | async-start | bytes 4259840 | tf_op jit(solution)/shard_map/all_gather | solution.py:47
  8.7 192.1 %all-gather.9.cloned.1.call-start = ((), (), s32[]{:S(2)}) async-start(), calls=%async_computation.4 | async-start | bytes 4718592 | tf_op jit(solution)/shard_map/all_gather | solution.py:60
  164.2 78.6 %all-gather.7.cloned.1.call-start = ((), (), s32[]{:S(2)}) async-start(), calls=%async_computation.3 | async-start | bytes 4718592 | tf_op jit(solution)/shard_map/all_gather | solution.py:60
  168.1 36.3 %copy-start.2 = (bf16[1,4096,128]{2,1,0:T(8,128)(2,1)S(1)}, bf16[1,4096,128]{2,1,0:T(8,128)(2,1)}, u32[]{:S(2)}) copy-start(bf16[1,4096,128]{2,1,0:T(8,128)(2,1)} %param.16) | copy-start | bytes 3145732
  168.1 129.0 %reduce-scatter.2.cloned.1.call-start = ((), (), s32[]{:S(2)}) async-start(), calls=%async_computation.5 | async-start | bytes 4718592 | tf_op jit(solution)/shard_map/reduce_scatter | solution.py:87
  200.8 3.6 copy-start.1
  254.0 29.8 %collective-permute-start = (bf16[128,4096]{1,0:T(8,128)(2,1)S(1)}, bf16[128,4096]{1,0:T(8,128)(2,1)S(1)}, u32[]{:S(2)}, u32[]{:S(2)}) collective-permute-start(bf16[128,4096]{1,0:T(8,128)(2,1)S(1)} %convolution_convert_fusion), channel_id=1, source_target_pairs={{0,1},{1,2},{2,3},{3,4},{4,5},{5,6},{6,7},{7,8},{8,9},{9,10},{10,1... | collective-permute-start | bytes 3145736 | tf_op jit(solution)/shard_map/ppermute | solution.py:12
  257.5 27.5 %collective-permute-start.2 = (bf16[128,4096]{1,0:T(8,128)(2,1)S(1)}, bf16[128,4096]{1,0:T(8,128)(2,1)}, u32[]{:S(2)}, u32[]{:S(2)}) collective-permute-start(bf16[128,4096]{1,0:T(8,128)(2,1)S(1)} %convolution_convert_fusion), channel_id=1, source_target_pairs={{0,63},{1,0},{2,1},{3,2},{4,3},{5,4},{6,5},{7,6},{8,7},{9,8},{10,9... | collective-permute-start | bytes 3145736 | tf_op jit(solution)/shard_map/ppermute | solution.py:12
  264.4 48.7 %copy-start.3 = (s32[32,8]{0,1:T(8,128)S(1)}, s32[32,8]{0,1:T(8,128)}, u32[]{:S(2)}) copy-start(s32[32,8]{0,1:T(8,128)} %param.12) | copy-start | bytes 3076
  264.4 48.8 %copy-start.4 = (s32[32,8]{0,1:T(8,128)S(1)}, s32[32,8]{0,1:T(8,128)}, u32[]{:S(2)}) copy-start(s32[32,8]{0,1:T(8,128)} %param.13) | copy-start | bytes 3076
  288.2 37.2 %collective-permute-start.1 = (bf16[128,4096]{1,0:T(8,128)(2,1)}, bf16[128,4096]{1,0:T(8,128)(2,1)}, u32[]{:S(2)}, u32[]{:S(2)}) collective-permute-start(bf16[128,4096]{1,0:T(8,128)(2,1)} %get-tuple-element.10), channel_id=1, source_target_pairs={{0,2},{1,3},{2,4},{3,5},{4,6},{5,7},{6,8},{7,9},{8,10},{9,11},{10,... | collective-permute-start | bytes 3145736 | tf_op jit(solution)/shard_map/ppermute | solution.py:12
  293.2 54.8 %collective-permute-start.3 = (bf16[128,4096]{1,0:T(8,128)(2,1)}, bf16[128,4096]{1,0:T(8,128)(2,1)}, u32[]{:S(2)}, u32[]{:S(2)}) collective-permute-start(bf16[128,4096]{1,0:T(8,128)(2,1)} %get-tuple-element.11), channel_id=1, source_target_pairs={{0,62},{1,63},{2,0},{3,1},{4,2},{5,3},{6,4},{7,5},{8,6},{9,7},{10,... | collective-permute-start | bytes 3145736 | tf_op jit(solution)/shard_map/ppermute | solution.py:12
  297.1 75.4 %all-to-all-start = ((bf16[64,8,512]{2,1,0:T(8,128)(2,1)}), bf16[64,8,512]{2,1,0:T(8,128)(2,1)}, u32[]{:S(2)}, u32[]{:S(2)}) async-start(bf16[64,8,512]{2,1,0:T(8,128)(2,1)} %reduce-scatter.2.cloned.1.call-done), calls=%async_computation.1 | async-start | bytes 1048576 | tf_op jit(solution)/shard_map/all_to_all | solution.py:90
Sparse Core Ops, SparseCore 0:
  11.5 148.9 all-gather.4
  164.4 36.4 all-gather.8
  202.9 39.8 all-gather.6
  251.2 45.8 reduce-scatter.1
